TPU v7x, 32 devices: a whole 2x2x4 slice. The times are simulated.
32 devices in a mesh: groups: 2 (over x), depth: 8 (over z, y), height: 2 (over core).
Axes of the slice: x: 2, y: 2, z: 4, core: 2. Of those that a mesh axis runs over, the one named last changes fastest.
Arguments:
- images: bfloat16 [4, 4, 64, 16, 256], P('groups', None, 'depth', 'height'), parts along dimension 0, may hold values from -6 to 6
- pre_hidden: bfloat16 [4, 16, 64, 16, 256], P('groups', None, 'depth', 'height'), parts along dimension 0, may hold values from -6 to 6
- pre_deep: bfloat16 [4, 32, 32, 8, 128], P(('groups', 'height'), None, 'depth'), parts along dimension 0, may hold values from -6 to 6
- pooled_grad: bfloat16 [4, 32, 16, 256], P(('groups', 'height'), None, 'depth'), parts along dimension 0, may hold values from -1.25 to 1.25
- deep_weight: bfloat16 [32, 16, 3, 3, 3], replicated, may hold values from -0.3125 to 0.3125
Outputs:
- first_kernel: float32 [32, 4, 3, 3, 3], P('groups'), parts along dimension 0
- first_bias: float32 [32], P('groups'), parts along dimension 0
- deep_kernel: float32 [64, 16, 3, 3, 3], P('groups'), parts along dimension 0
- deep_bias: float32 [64], P('groups'), parts along dimension 0
There are 2 independent parts, one for each index of `groups`. A program takes and returns all parts, laid end to end along the dimension named above; an argument that names none is the same for every part. Nothing has to cross between parts.
All inputs are finite; a program needn't handle non-finite values.
Results may differ from a plain program's by a relative error of at most 0.0031.
Values may be sent and summed in bfloat16 or wider, within the bound.
A program may use at most 128 MiB of HBM per device.

v0:
```python
import jax
import jax.numpy as jnp
from jax import lax
from jax.sharding import PartitionSpec as P

SLOPE = 0.3


def padded_2(block, sides, width):
    for axis, dim in sides:
        count = lax.axis_size(axis)
        forward = [(i, i + 1) for i in range(count - 1)]
        backward = [(target, source) for source, target in forward]
        low = lax.ppermute(
            lax.slice_in_dim(block, block.shape[dim] - width, None, axis=dim), axis, forward
        )
        high = lax.ppermute(lax.slice_in_dim(block, 0, width, axis=dim), axis, backward)
        block = jnp.concatenate([low, block, high], axis=dim)
    return block


def from_behind(value, axis, steps):
    count = lax.axis_size(axis)
    leading, last = (max(0, -steps), min(count, count - steps))
    return lax.ppermute(value, axis, [(source, source + steps) for source in range(leading, last)])


def leaky(values):
    return jnp.where(values > 0, values, SLOPE * values)


def slope_at(values):
    return jnp.where(values > 0, 1.0, SLOPE)


def deep_gradient(pooled_grad, pre_deep):
    samples, chans, quarter, flat = pooled_grad.shape
    half_depth, half_height, half_width = (pre_deep.shape[2], pre_deep.shape[3], pre_deep.shape[4])
    coarse = (
        pooled_grad.astype(jnp.float32).reshape(
            samples, chans, quarter, 1, half_height // 2, 1, half_width // 2, 1
        )
        / 8.0
    )
    spread = jnp.broadcast_to(
        coarse, (samples, chans, quarter, 2, half_height // 2, 2, half_width // 2, 2)
    )
    spread = spread.reshape(samples, chans, half_depth, half_height, half_width)
    return (spread * slope_at(pre_deep.astype(jnp.float32))).astype(jnp.bfloat16)


def deep_weight_grad(local_grad, padded):
    samples, chans = (padded.shape[0], padded.shape[1])
    coarse_depth, coarse_height, coarse_width = (
        local_grad.shape[2],
        local_grad.shape[3],
        local_grad.shape[4],
    )
    grown = jnp.pad(padded, ((0, 0), (0, 0), (0, 1), (0, 1), (0, 1)))
    phases = grown.reshape(
        samples, chans, coarse_depth + 1, 2, coarse_height + 1, 2, coarse_width + 1, 2
    )
    phases = phases.transpose(0, 1, 3, 5, 7, 2, 4, 6)
    kernels = []
    for depth_tap in range(3):
        for height_tap in range(3):
            for width_tap in range(3):
                depth_off, height_off, width_off = (depth_tap // 2, height_tap // 2, width_tap // 2)
                view = phases[
                    :,
                    :,
                    depth_tap % 2,
                    height_tap % 2,
                    width_tap % 2,
                    depth_off : depth_off + coarse_depth,
                    height_off : height_off + coarse_height,
                    width_off : width_off + coarse_width,
                ]
                kernels.append(
                    jnp.einsum(
                        "sodhw,sidhw->oi", local_grad, view, preferred_element_type=jnp.float32
                    )
                )
    kernel = jnp.stack(kernels, axis=-1).reshape(local_grad.shape[1], chans, 3, 3, 3)
    return (kernel, jnp.sum(local_grad, axis=(0, 2, 3, 4), dtype=jnp.float32))


def transpose_conv(extended, deep_weight):
    samples = extended.shape[0]
    coarse_depth, coarse_height, coarse_width = (
        extended.shape[2] - 1,
        extended.shape[3] - 1,
        extended.shape[4] - 1,
    )
    out_chans = deep_weight.shape[1]
    phase_taps = (((1, 0),), ((2, 0), (0, 1)))
    phases = []
    for depth_phase in range(2):
        for height_phase in range(2):
            for width_phase in range(2):
                views = []
                mats = []
                for depth_tap, depth_step in phase_taps[depth_phase]:
                    for height_tap, height_step in phase_taps[height_phase]:
                        for width_tap, width_step in phase_taps[width_phase]:
                            views.append(
                                extended[
                                    :,
                                    :,
                                    depth_step : depth_step + coarse_depth,
                                    height_step : height_step + coarse_height,
                                    width_step : width_step + coarse_width,
                                ]
                            )
                            mats.append(deep_weight[:, :, depth_tap, height_tap, width_tap])
                stacked = jnp.concatenate(views, axis=1)
                matrix = jnp.concatenate(mats, axis=0)
                phases.append(
                    jnp.einsum(
                        "sodhw,oi->sidhw", stacked, matrix, preferred_element_type=jnp.float32
                    )
                )
    grid = jnp.stack(phases, axis=0).reshape(
        2, 2, 2, samples, out_chans, coarse_depth, coarse_height, coarse_width
    )
    woven = grid.transpose(3, 4, 5, 0, 6, 1, 7, 2).reshape(
        samples, out_chans, 2 * coarse_depth, 2 * coarse_height, 2 * coarse_width
    )
    return woven.astype(jnp.bfloat16)


def first_weight_grad(first_grad, framed):
    chans = framed.shape[1]
    cells_depth, cells_height, cells_width = (
        first_grad.shape[2],
        first_grad.shape[3],
        first_grad.shape[4],
    )
    kernels = []
    for depth_tap in range(3):
        for height_tap in range(3):
            for width_tap in range(3):
                view = framed[
                    :,
                    :,
                    depth_tap : depth_tap + cells_depth,
                    height_tap : height_tap + cells_height,
                    width_tap : width_tap + cells_width,
                ]
                kernels.append(
                    jnp.einsum(
                        "sodhw,sidhw->oi", first_grad, view, preferred_element_type=jnp.float32
                    )
                )
    kernel = jnp.stack(kernels, axis=-1).reshape(first_grad.shape[1], chans, 3, 3, 3)
    return (kernel, jnp.sum(first_grad, axis=(0, 2, 3, 4), dtype=jnp.float32))


def on_device(images, pre_hidden, pre_deep, pooled_grad, deep_weight):
    deep_grad = deep_gradient(pooled_grad, pre_deep)
    hidden = leaky(pre_hidden.astype(jnp.float32)).astype(jnp.bfloat16)
    bordered = padded_2(images, (("depth", 2), ("height", 3)), 1)
    framed = jnp.pad(bordered, ((0, 0), (0, 0), (0, 0), (0, 0), (1, 1)))
    gathered = lax.all_to_all(hidden, "height", split_axis=0, concat_axis=3, tiled=True)
    below = from_behind(gathered[:, :, -1:], "depth", 1)
    padded = jnp.pad(
        jnp.concatenate([below, gathered], axis=2), ((0, 0), (0, 0), (0, 0), (1, 0), (1, 0))
    )
    above = from_behind(deep_grad[:, :, :1], "depth", -1)
    extended = jnp.pad(
        jnp.concatenate([deep_grad, above], axis=2), ((0, 0), (0, 0), (0, 0), (0, 1), (0, 1))
    )
    returned = transpose_conv(extended, deep_weight)
    hidden_grad = lax.all_to_all(returned, "height", split_axis=3, concat_axis=0, tiled=True)
    deep_kernel, deep_bias = deep_weight_grad(deep_grad, padded)
    first_grad = (
        hidden_grad.astype(jnp.float32) * slope_at(pre_hidden.astype(jnp.float32))
    ).astype(jnp.bfloat16)
    first_kernel, first_bias = first_weight_grad(first_grad, framed)
    first_kernel, first_bias, deep_kernel, deep_bias = lax.psum(
        (first_kernel, first_bias, deep_kernel, deep_bias), ("depth", "height")
    )
    return (first_kernel, first_bias, deep_kernel, deep_bias)


def solution(mesh):
    return jax.shard_map(
        on_device,
        mesh=mesh,
        in_specs=(
            P("groups", None, "depth", "height", None),
            P("groups", None, "depth", "height", None),
            P(("groups", "height"), None, "depth", None, None),
            P(("groups", "height"), None, "depth", None),
            P(),
        ),
        out_specs=(
            P("groups", None, None, None, None),
            P("groups"),
            P("groups", None, None, None, None),
            P("groups"),
        ),
        check_vma=False,
    )
```

profile of v0, /device:TPU:0, one launch (start us, length us, event | category | flops | bytes accessed | tf_op | source)
XLA Modules:
  0.0 230.6 jit_solution(8759666628445355263)
XLA Ops:
  0.6 1.2 copy.92
  2.5 1.3 collective-permute-start.2
  3.8 6.1 %collective-permute-start.1 = (bf16[2,4,1,8,256]{4,1,0,3,2:T(4,128)(2,1)}, bf16[2,4,1,8,256]{4,1,0,3,2:T(4,128)(2,1)}, u32[]{:S(2)}, u32[]{:S(2)}) collective-permute-start(bf16[2,4,1,8,256]{4,1,0,3,2:T(4,128)(2,1)} %get-tuple-element.24), channel_id=1, source_target_pairs={{0,2},{2,4},{4,6},{6,8},{8,10},{10,12},{12,14},{1,3},{3,5},{5,7},{... | collective-permute-start | bytes 98312 | tf_op jit(solution)/shard_map/ppermute | solution.py:14
  10.9 0.9 broadcast_in_dim.23
  13.2 1.3 collective-permute-start
  18.3 1.2 constant_dynamic-update-slice_fusion.8
  21.0 2.1 collective-permute-start.3
  23.0 1.3 collective-permute-start.4
  28.2 14.3 %copy.88 = bf16[2,2,2,1,16,4,8,128]{4,2,7,1,6,0,5,3:T(2,128)(2,1)} copy(bf16[2,2,2,1,16,4,8,128]{7,4,6,5,2,1,0,3:T(8,128)(2,1)S(1)} %bitcast.783) | data formatting | bytes 2097152 | tf_op jit(solution)/shard_map/convert_element_type | solution.py:129
  42.5 6.9 %copy.89 = bf16[1,16,8,16,256]{4,2,1,0,3:T(8,128)(2,1)S(1)} copy(bf16[1,16,8,16,256]{1,4,3,2,0:T(8,128)(2,1)} %bitcast.752) | data formatting | bytes 2097152 | tf_op jit(solution)/shard_map/convert_element_type | solution.py:129
  49.4 5.9 %all_to_all.27 = bf16[1,16,8,16,256]{4,2,1,0,3:T(8,128)(2,1)S(1)} all-to-all(bf16[1,16,8,16,256]{4,2,1,0,3:T(8,128)(2,1)S(1)} %copy.89), channel_id=1, replica_groups=mesh['groups'=2,'depth'=8,'height'=2] {'height'}, dimensions={3} | all-to-all | bytes 2097152 | tf_op jit(solution)/shard_map/all_to_all | solution.py:174
  55.3 1.3 convert_reduce_fusion
  56.8 4.7 %all_to_all.28 = bf16[2,16,8,8,256]{4,3,2,1,0:T(8,128)(2,1)S(1)} all-to-all(bf16[2,16,8,8,256]{4,3,2,1,0:T(8,128)(2,1)S(1)} %copy.125), channel_id=1, replica_groups=mesh['groups'=2,'depth'=8,'height'=2] {'height'}, dimensions={0} | all-to-all | bytes 2097152 | tf_op jit(solution)/shard_map/all_to_all | solution.py:164
  61.6 4.9 %collective-permute-start.5 = (bf16[1,16,1,16,256]{4,3,2,1,0:T(8,128)(2,1)S(1)}, bf16[1,16,1,16,256]{4,3,2,1,0:T(8,128)(2,1)S(1)}, u32[]{:S(2)}, u32[]{:S(2)}) collective-permute-start(bf16[1,16,1,16,256]{4,3,2,1,0:T(8,128)(2,1)S(1)} %slice.448), channel_id=1, source_target_pairs={{0,2},{2,4},{4,6},{6,8},{8,10},{10,12},{12,14},{1,3},{3,5},{5,7},{... | collective-permute-start | bytes 393224 | tf_op jit(solution)/shard_map/ppermute | solution.py:25
  66.5 1.4 select_maximum_fusion
  68.7 1.6 fusion.81
  70.3 0.9 fusion.80
  72.0 1.6 fusion.78
  75.2 1.6 fusion.75
  76.8 0.9 fusion.74
  78.5 1.6 fusion.72
  80.1 0.9 fusion.71
  81.8 0.9 fusion.69
  84.4 1.8 fusion.66
  87.9 1.6 fusion.63
  91.1 1.6 fusion.60
  94.4 1.6 fusion.57
  97.0 6.6 %copy.193 = bf16[1,16,9,16,256]{1,4,3,2,0:T(8,128)(2,1)} copy(bf16[1,16,9,16,256]{4,3,2,1,0:T(8,128)(2,1)S(1)} %pad_maximum_fusion.4) | data formatting | bytes 2359296
  103.6 10.9 %pad.82 = bf16[1,16,10,18,258]{1,4,3,2,0:T(8,128)(2,1)} pad(bf16[1,16,9,16,256]{1,4,3,2,0:T(8,128)(2,1)} %copy.193, bf16[]{:T(256)} %constant.3.clone.1), padding=0_0x0_0x0_1x1_1x1_1 | pad | bytes 2665730 | tf_op jit(solution)/shard_map/jit(_pad)/pad | solution.py:59
  114.5 24.0 %reshape.237 = bf16[1,16,5,2,9,2,129,2]{1,7,6,5,4,3,2,0:T(2,128)(2,1)} reshape(bf16[1,16,10,18,258]{1,4,3,2,0:T(8,128)(2,1)} %pad.82) | data formatting | bytes 2972160 | tf_op jit(solution)/shard_map/reshape | solution.py:60
  138.5 22.6 %copy.128 = bf16[1,16,5,2,9,2,129,2]{6,1,4,2,7,5,3,0:T(8,128)(2,1)S(1)} copy(bf16[1,16,5,2,9,2,129,2]{1,7,6,5,4,3,2,0:T(2,128)(2,1)} %reshape.237) | data formatting | bytes 2972160 | tf_op jit(solution)/shard_map/reshape | solution.py:60
  166.9 63.7 %all-reduce.4 = (f32[16,4,3,3,3]{0,1,4,3,2:T(4,128)}, f32[16]{0:T(128)}, f32[32,16,3,3,3]{0,1,4,3,2:T(8,128)}, f32[32]{0:T(128)}) all-reduce(f32[16,4,3,3,3]{0,1,4,3,2:T(4,128)S(1)} %bitcast.786, f32[16]{0:T(128)S(1)} %get-tuple-element.10, ...), channel_id=1, replica_groups=mesh['groups'=2,'depth'=8,'height'=2] {'depth','height'}, use_global_device_ids=true, to_apply=%region_0.1 | all-reduce | flops 15600 | bytes 124800 | tf_op jit(solution)/shard_map/psum | solution.py:180
  (135 shorter events, 30.4 us)
Async XLA Ops:
  1.8 8.1 %copy-start.4 = (bf16[2,4,8,8,256]{4,1,0,3,2:T(4,128)(2,1)}, bf16[2,4,8,8,256]{4,1,0,3,2:T(4,128)(2,1)S(1)}, u32[]{:S(2)}) copy-start(bf16[2,4,8,8,256]{4,1,0,3,2:T(4,128)(2,1)S(1)} %copy.92) | copy-start | bytes 786436
  2.5 16.9 %collective-permute-start.2 = (bf16[2,4,1,8,256]{4,1,0,3,2:T(4,128)(2,1)}, bf16[2,4,1,8,256]{4,1,0,3,2:T(4,128)(2,1)}, u32[]{:S(2)}, u32[]{:S(2)}) collective-permute-start(bf16[2,4,1,8,256]{4,1,0,3,2:T(4,128)(2,1)} %get-tuple-element.23), channel_id=1, source_target_pairs={{2,0},{4,2},{6,4},{8,6},{10,8},{12,10},{14,12},{3,1},{5,3},{7,5},{... | collective-permute-start | bytes 98312 | tf_op jit(solution)/shard_map/ppermute | solution.py:17
  3.8 13.7 %collective-permute-start.1 = (bf16[2,4,1,8,256]{4,1,0,3,2:T(4,128)(2,1)}, bf16[2,4,1,8,256]{4,1,0,3,2:T(4,128)(2,1)}, u32[]{:S(2)}, u32[]{:S(2)}) collective-permute-start(bf16[2,4,1,8,256]{4,1,0,3,2:T(4,128)(2,1)} %get-tuple-element.24), channel_id=1, source_target_pairs={{0,2},{2,4},{4,6},{6,8},{8,10},{10,12},{12,14},{1,3},{3,5},{5,7},{... | collective-permute-start | bytes 98312 | tf_op jit(solution)/shard_map/ppermute | solution.py:14
  10.9 1.5 copy-start.6
  11.8 2.7 %copy-start.7 = (bf16[32,16,3,3,3]{0,1,4,3,2:T(8,128)(2,1)S(1)}, bf16[32,16,3,3,3]{0,1,4,3,2:T(8,128)(2,1)}, u32[]{:S(2)}) copy-start(bf16[32,16,3,3,3]{0,1,4,3,2:T(8,128)(2,1)} %param.9) | copy-start | bytes 82948
  13.2 11.2 %collective-permute-start = (bf16[1,32,1,8,128]{4,1,3,2,0:T(8,128)(2,1)S(1)}, bf16[1,32,1,8,128]{4,1,3,2,0:T(8,128)(2,1)S(1)}, u32[]{:S(2)}, u32[]{:S(2)}) collective-permute-start(bf16[1,32,1,8,128]{4,1,3,2,0:T(8,128)(2,1)S(1)} %slice.415), channel_id=1, source_target_pairs={{2,0},{4,2},{6,4},{8,6},{10,8},{12,10},{14,12},{3,1},{5,3},{7,5},{... | collective-permute-start | bytes 196616 | tf_op jit(solution)/shard_map/ppermute | solution.py:25
  20.2 4.9 %copy-start.2 = (bf16[2,4,10,8,256]{4,1,0,3,2:T(4,128)(2,1)}, bf16[2,4,10,8,256]{4,1,0,3,2:T(4,128)(2,1)S(1)}, u32[]{:S(2)}) copy-start(bf16[2,4,10,8,256]{4,1,0,3,2:T(4,128)(2,1)S(1)} %constant_dynamic-update-slice_fusion.7) | copy-start | bytes 983044
  21.0 45.5 %collective-permute-start.3 = (bf16[2,4,10,1,256]{4,1,0,3,2:T(4,128)(2,1)}, bf16[2,4,10,1,256]{4,1,0,3,2:T(4,128)(2,1)}, u32[]{:S(2)}, u32[]{:S(2)}) collective-permute-start(bf16[2,4,10,1,256]{4,1,0,3,2:T(4,128)(2,1)} %get-tuple-element.21), channel_id=1, source_target_pairs={{0,1},{2,3},{4,5},{6,7},{8,9},{10,11},{12,13},{14,15},{16,17},{18,... | collective-permute-start | bytes 122888 | tf_op jit(solution)/shard_map/ppermute | solution.py:14
  23.0 43.5 %collective-permute-start.4 = (bf16[2,4,10,1,256]{4,1,0,3,2:T(4,128)(2,1)}, bf16[2,4,10,1,256]{4,1,0,3,2:T(4,128)(2,1)}, u32[]{:S(2)}, u32[]{:S(2)}) collective-permute-start(bf16[2,4,10,1,256]{4,1,0,3,2:T(4,128)(2,1)} %get-tuple-element.22), channel_id=1, source_target_pairs={{1,0},{3,2},{5,4},{7,6},{9,8},{11,10},{13,12},{15,14},{17,16},{19,... | collective-permute-start | bytes 122888 | tf_op jit(solution)/shard_map/ppermute | solution.py:17
  24.8 0.9 copy-start.12
  24.8 0.9 copy-start.13
  24.9 1.1 copy-start.10
  24.9 1.1 copy-start.11
  25.1 1.2 copy-start.8
  25.2 1.2 copy-start.9
  25.2 1.2 copy-start.24
  25.2 1.2 copy-start.25
  26.0 0.7 copy-start.22
  26.1 0.7 copy-start.23
  26.4 0.7 copy-start.18
  26.4 0.7 copy-start.19
  26.4 0.7 copy-start.20
  26.4 0.7 copy-start.21
  26.8 0.7 copy-start.14
  26.8 0.7 copy-start.15
  26.8 0.7 copy-start.16
  49.4 5.9 %copy-start = (bf16[2,16,8,8,256]{4,3,2,1,0:T(8,128)(2,1)S(1)}, bf16[2,16,8,8,256]{4,3,2,1,0:T(8,128)(2,1)}, u32[]{:S(2)}) copy-start(bf16[2,16,8,8,256]{4,3,2,1,0:T(8,128)(2,1)} %param.6) | copy-start | bytes 3145732
  56.8 9.7 %copy-start.3 = (bf16[2,4,10,8,256]{4,1,0,3,2:T(4,128)(2,1)S(1)}, bf16[2,4,10,8,256]{4,1,0,3,2:T(4,128)(2,1)}, u32[]{:S(2)}) copy-start(bf16[2,4,10,8,256]{4,1,0,3,2:T(4,128)(2,1)} %copy-done.2) | copy-start | bytes 983044
  61.6 35.3 %collective-permute-start.5 = (bf16[1,16,1,16,256]{4,3,2,1,0:T(8,128)(2,1)S(1)}, bf16[1,16,1,16,256]{4,3,2,1,0:T(8,128)(2,1)S(1)}, u32[]{:S(2)}, u32[]{:S(2)}) collective-permute-start(bf16[1,16,1,16,256]{4,3,2,1,0:T(8,128)(2,1)S(1)} %slice.448), channel_id=1, source_target_pairs={{0,2},{2,4},{4,6},{6,8},{8,10},{10,12},{12,14},{1,3},{3,5},{5,7},{... | collective-permute-start | bytes 393224 | tf_op jit(solution)/shard_map/ppermute | solution.py:25
  70.3 1.7 copy-start.5
  80.1 1.7 copy-start.1
  164.7 2.2 copy-start.26
  (1 other events, 0.7 us)
where the time goes:
time: 233 us; the launch traced here: 231 us
  local copies, waits for them, and re-layouts  95.9 us (41%)
  blocking collectives  74.3 us (32%)
  matrix products  37.7 us (16%)
  starting transfers between devices  16.9 us (7%)
  other arithmetic  4.49 us (2%)
    psum x1, blocking collectives, on_device(): lax.psum((first_kernel, first_bias, deep_kernel, deep_bias), ('depth', 'h...  63.7 us
    reshape x2, local copies, waits for them, and re-layouts, deep_weight_grad(): grown.reshape(samples, chans, coarse_depth + 1, 2, coarse_height + 1, 2,...  46.6 us
    dot_general x27, matrix products, first_weight_grad(): jnp.einsum('sodhw,sidhw->oi', first_grad, view, preferred_element_type=jn...  29 us
    convert_element_type x2, local copies, waits for them, and re-layouts, transpose_conv(): return woven.astype(jnp.bfloat16)  21.2 us
    pad x1, local copies, waits for them, and re-layouts, deep_weight_grad(): grown = jnp.pad(padded, ((0, 0), (0, 0), (0, 1), (0, 1), (0, 1)))  10.9 us
    unnamed x64, local copies, waits for them, and re-layouts  10.4 us
    ppermute x2, starting transfers between devices, padded_2(): lax.ppermute(lax.slice_in_dim(block, block.shape[dim] - width, None, axis...  8.18 us
    ppermute x2, starting transfers between devices, from_behind(): lax.ppermute(value, axis, [(source, source + steps) for source in range(l...  6.15 us
  transfers between devices with their start and end apart: 6, of which 0 were waited for; matrix products, arithmetic and copies ran while one was open for 29% of the time, Pallas kernels for 0%

commit v1 on v0

--- a/solution.py
+++ b/solution.py
@@ -4,6 +4,11 @@
 from jax.sharding import PartitionSpec as P
 
 SLOPE = 0.3
+
+
+def by_each_axis(array, one, other):
+    half = lax.psum(array, one)
+    return lax.psum(half, other)
 
 
 def padded_2(block, sides, width):
@@ -177,8 +182,8 @@
         hidden_grad.astype(jnp.float32) * slope_at(pre_hidden.astype(jnp.float32))
     ).astype(jnp.bfloat16)
     first_kernel, first_bias = first_weight_grad(first_grad, framed)
-    first_kernel, first_bias, deep_kernel, deep_bias = lax.psum(
-        (first_kernel, first_bias, deep_kernel, deep_bias), ("depth", "height")
+    first_kernel, first_bias, deep_kernel, deep_bias = by_each_axis(
+        (first_kernel, first_bias, deep_kernel, deep_bias), "height", "depth"
     )
     return (first_kernel, first_bias, deep_kernel, deep_bias)
 

time: 233 us -> 214 us (0.918)
  blocking collectives: 74.3 us -> 54.7 us
    psum x1 -> x2, blocking collectives: 63.7 us -> 44.1 us  [the longest x1 40 us: by_each_axis(): return lax.psum(half, other)]
  transfers between devices with their start and end apart: 6 -> 6, of which waited for: 0 -> 0; matrix products, arithmetic and copies ran while one was open for 29% -> 31% of each run, Pallas kernels for 0% -> 0%
where the time goes in v1:
time: 214 us; the launch traced here: 211 us
  local copies, waits for them, and re-layouts  95.9 us (45%)
  blocking collectives  54.7 us (26%)
  matrix products  37.7 us (18%)
  starting transfers between devices  16.9 us (8%)
  other arithmetic  4.49 us (2%)
    reshape x2, local copies, waits for them, and re-layouts, deep_weight_grad(): grown.reshape(samples, chans, coarse_depth + 1, 2, coarse_height + 1, 2,...  46.6 us
    psum x1, blocking collectives, by_each_axis(): return lax.psum(half, other)  40 us
    dot_general x27, matrix products, first_weight_grad(): jnp.einsum('sodhw,sidhw->oi', first_grad, view, preferred_element_type=jn...  29 us
    convert_element_type x2, local copies, waits for them, and re-layouts, transpose_conv(): return woven.astype(jnp.bfloat16)  21.2 us
    pad x1, local copies, waits for them, and re-layouts, deep_weight_grad(): grown = jnp.pad(padded, ((0, 0), (0, 0), (0, 1), (0, 1), (0, 1)))  10.9 us
    unnamed x64, local copies, waits for them, and re-layouts  10.4 us
    ppermute x2, starting transfers between devices, padded_2(): lax.ppermute(lax.slice_in_dim(block, block.shape[dim] - width, None, axis...  8.18 us
    ppermute x2, starting transfers between devices, from_behind(): lax.ppermute(value, axis, [(source, source + steps) for source in range(l...  6.15 us
  transfers between devices with their start and end apart: 6, of which 0 were waited for; matrix products, arithmetic and copies ran while one was open for 31% of the time, Pallas kernels for 0%

profile of v1, /device:TPU:0, one launch (start us, length us, event | category | flops | bytes accessed | tf_op | source)
XLA Modules:
  0.0 210.9 jit_solution(17524903641963530051)
XLA Ops:
  0.6 1.2 copy.92
  2.5 1.3 collective-permute-start.2
  3.8 6.1 %collective-permute-start.1 = (bf16[2,4,1,8,256]{4,1,0,3,2:T(4,128)(2,1)}, bf16[2,4,1,8,256]{4,1,0,3,2:T(4,128)(2,1)}, u32[]{:S(2)}, u32[]{:S(2)}) collective-permute-start(bf16[2,4,1,8,256]{4,1,0,3,2:T(4,128)(2,1)} %get-tuple-element.28), channel_id=1, source_target_pairs={{0,2},{2,4},{4,6},{6,8},{8,10},{10,12},{12,14},{1,3},{3,5},{5,7},{... | collective-permute-start | bytes 98312 | tf_op jit(solution)/shard_map/ppermute | solution.py:19
  10.9 0.9 broadcast_in_dim.23
  13.2 1.3 collective-permute-start
  18.2 1.2 constant_dynamic-update-slice_fusion.8
  21.0 2.1 collective-permute-start.3
  23.0 1.3 collective-permute-start.4
  28.2 14.4 %copy.88 = bf16[2,2,2,1,16,4,8,128]{4,2,7,1,6,0,5,3:T(2,128)(2,1)} copy(bf16[2,2,2,1,16,4,8,128]{7,4,6,5,2,1,0,3:T(8,128)(2,1)S(1)} %bitcast.783) | data formatting | bytes 2097152 | tf_op jit(solution)/shard_map/convert_element_type | solution.py:134
  42.6 6.9 %copy.89 = bf16[1,16,8,16,256]{4,2,1,0,3:T(8,128)(2,1)S(1)} copy(bf16[1,16,8,16,256]{1,4,3,2,0:T(8,128)(2,1)} %bitcast.752) | data formatting | bytes 2097152 | tf_op jit(solution)/shard_map/convert_element_type | solution.py:134
  49.4 5.9 %all_to_all.27 = bf16[1,16,8,16,256]{4,2,1,0,3:T(8,128)(2,1)S(1)} all-to-all(bf16[1,16,8,16,256]{4,2,1,0,3:T(8,128)(2,1)S(1)} %copy.89), channel_id=1, replica_groups=mesh['groups'=2,'depth'=8,'height'=2] {'height'}, dimensions={3} | all-to-all | bytes 2097152 | tf_op jit(solution)/shard_map/all_to_all | solution.py:179
  55.4 1.3 convert_reduce_fusion
  56.8 4.7 %all_to_all.28 = bf16[2,16,8,8,256]{4,3,2,1,0:T(8,128)(2,1)S(1)} all-to-all(bf16[2,16,8,8,256]{4,3,2,1,0:T(8,128)(2,1)S(1)} %copy.125), channel_id=1, replica_groups=mesh['groups'=2,'depth'=8,'height'=2] {'height'}, dimensions={0} | all-to-all | bytes 2097152 | tf_op jit(solution)/shard_map/all_to_all | solution.py:169
  61.7 4.9 %collective-permute-start.5 = (bf16[1,16,1,16,256]{4,3,2,1,0:T(8,128)(2,1)S(1)}, bf16[1,16,1,16,256]{4,3,2,1,0:T(8,128)(2,1)S(1)}, u32[]{:S(2)}, u32[]{:S(2)}) collective-permute-start(bf16[1,16,1,16,256]{4,3,2,1,0:T(8,128)(2,1)S(1)} %slice.448), channel_id=1, source_target_pairs={{0,2},{2,4},{4,6},{6,8},{8,10},{10,12},{12,14},{1,3},{3,5},{5,7},{... | collective-permute-start | bytes 393224 | tf_op jit(solution)/shard_map/ppermute | solution.py:30
  66.6 1.4 select_maximum_fusion
  68.7 1.6 fusion.81
  70.3 0.9 fusion.80
  72.0 1.6 fusion.78
  75.3 1.6 fusion.75
  76.9 0.9 fusion.74
  78.6 1.6 fusion.72
  81.9 0.9 fusion.69
  84.4 1.8 fusion.66
  87.9 1.6 fusion.63
  91.2 1.6 fusion.60
  94.5 1.6 fusion.57
  97.1 6.5 %copy.193 = bf16[1,16,9,16,256]{1,4,3,2,0:T(8,128)(2,1)} copy(bf16[1,16,9,16,256]{4,3,2,1,0:T(8,128)(2,1)S(1)} %pad_maximum_fusion.4) | data formatting | bytes 2359296
  103.5 10.9 %pad.82 = bf16[1,16,10,18,258]{1,4,3,2,0:T(8,128)(2,1)} pad(bf16[1,16,9,16,256]{1,4,3,2,0:T(8,128)(2,1)} %copy.193, bf16[]{:T(256)} %constant.3.clone.1), padding=0_0x0_0x0_1x1_1x1_1 | pad | bytes 2665730 | tf_op jit(solution)/shard_map/jit(_pad)/pad | solution.py:64
  114.5 24.0 %reshape.237 = bf16[1,16,5,2,9,2,129,2]{1,7,6,5,4,3,2,0:T(2,128)(2,1)} reshape(bf16[1,16,10,18,258]{1,4,3,2,0:T(8,128)(2,1)} %pad.82) | data formatting | bytes 2972160 | tf_op jit(solution)/shard_map/reshape | solution.py:65
  138.5 22.6 %copy.128 = bf16[1,16,5,2,9,2,129,2]{6,1,4,2,7,5,3,0:T(8,128)(2,1)S(1)} copy(bf16[1,16,5,2,9,2,129,2]{1,7,6,5,4,3,2,0:T(2,128)(2,1)} %reshape.237) | data formatting | bytes 2972160 | tf_op jit(solution)/shard_map/reshape | solution.py:65
  166.9 4.0 %all-reduce.5 = (f32[16,4,3,3,3]{0,1,4,3,2:T(4,128)S(1)}, f32[16]{0:T(128)S(1)}, f32[32,16,3,3,3]{0,1,4,3,2:T(8,128)S(1)}, f32[32]{0:T(128)S(1)}) all-reduce(f32[16,4,3,3,3]{0,1,4,3,2:T(4,128)S(1)} %bitcast.786, f32[16]{0:T(128)S(1)} %get-tuple-element.14, ...), channel_id=1, replica_groups=mesh['groups'=2,'depth'=8,'height'=2] {'height'}, use_global_device_ids=true, to_apply=%region_0.1 | all-reduce | flops 15600 | bytes 124800 | tf_op jit(solution)/shard_map/psum | solution.py:10
  170.9 40.0 %all-reduce.4 = (f32[16,4,3,3,3]{0,1,4,3,2:T(4,128)}, f32[16]{0:T(128)}, f32[32,16,3,3,3]{0,1,4,3,2:T(8,128)}, f32[32]{0:T(128)}) all-reduce(f32[16,4,3,3,3]{0,1,4,3,2:T(4,128)S(1)} %get-tuple-element.8, f32[16]{0:T(128)S(1)} %get-tuple-element.9, ...), channel_id=1, replica_groups=mesh['groups'=2,'depth'=8,'height'=2] {'depth'}, use_global_device_ids=true, to_apply=%region_1.2 | all-reduce | flops 15600 | bytes 124800 | tf_op jit(solution)/shard_map/psum | solution.py:11
  (136 shorter events, 31.3 us)
Async XLA Ops:
  1.8 8.1 %copy-start.4 = (bf16[2,4,8,8,256]{4,1,0,3,2:T(4,128)(2,1)}, bf16[2,4,8,8,256]{4,1,0,3,2:T(4,128)(2,1)S(1)}, u32[]{:S(2)}) copy-start(bf16[2,4,8,8,256]{4,1,0,3,2:T(4,128)(2,1)S(1)} %copy.92) | copy-start | bytes 786436
  2.5 16.9 %collective-permute-start.2 = (bf16[2,4,1,8,256]{4,1,0,3,2:T(4,128)(2,1)}, bf16[2,4,1,8,256]{4,1,0,3,2:T(4,128)(2,1)}, u32[]{:S(2)}, u32[]{:S(2)}) collective-permute-start(bf16[2,4,1,8,256]{4,1,0,3,2:T(4,128)(2,1)} %get-tuple-element.27), channel_id=1, source_target_pairs={{2,0},{4,2},{6,4},{8,6},{10,8},{12,10},{14,12},{3,1},{5,3},{7,5},{... | collective-permute-start | bytes 98312 | tf_op jit(solution)/shard_map/ppermute | solution.py:22
  3.8 13.7 %collective-permute-start.1 = (bf16[2,4,1,8,256]{4,1,0,3,2:T(4,128)(2,1)}, bf16[2,4,1,8,256]{4,1,0,3,2:T(4,128)(2,1)}, u32[]{:S(2)}, u32[]{:S(2)}) collective-permute-start(bf16[2,4,1,8,256]{4,1,0,3,2:T(4,128)(2,1)} %get-tuple-element.28), channel_id=1, source_target_pairs={{0,2},{2,4},{4,6},{6,8},{8,10},{10,12},{12,14},{1,3},{3,5},{5,7},{... | collective-permute-start | bytes 98312 | tf_op jit(solution)/shard_map/ppermute | solution.py:19
  10.9 1.5 copy-start.6
  11.8 2.7 %copy-start.7 = (bf16[32,16,3,3,3]{0,1,4,3,2:T(8,128)(2,1)S(1)}, bf16[32,16,3,3,3]{0,1,4,3,2:T(8,128)(2,1)}, u32[]{:S(2)}) copy-start(bf16[32,16,3,3,3]{0,1,4,3,2:T(8,128)(2,1)} %param.9) | copy-start | bytes 82948
  13.2 11.2 %collective-permute-start = (bf16[1,32,1,8,128]{4,1,3,2,0:T(8,128)(2,1)S(1)}, bf16[1,32,1,8,128]{4,1,3,2,0:T(8,128)(2,1)S(1)}, u32[]{:S(2)}, u32[]{:S(2)}) collective-permute-start(bf16[1,32,1,8,128]{4,1,3,2,0:T(8,128)(2,1)S(1)} %slice.415), channel_id=1, source_target_pairs={{2,0},{4,2},{6,4},{8,6},{10,8},{12,10},{14,12},{3,1},{5,3},{7,5},{... | collective-permute-start | bytes 196616 | tf_op jit(solution)/shard_map/ppermute | solution.py:30
  20.2 4.9 %copy-start.2 = (bf16[2,4,10,8,256]{4,1,0,3,2:T(4,128)(2,1)}, bf16[2,4,10,8,256]{4,1,0,3,2:T(4,128)(2,1)S(1)}, u32[]{:S(2)}) copy-start(bf16[2,4,10,8,256]{4,1,0,3,2:T(4,128)(2,1)S(1)} %constant_dynamic-update-slice_fusion.7) | copy-start | bytes 983044
  21.0 45.6 %collective-permute-start.3 = (bf16[2,4,10,1,256]{4,1,0,3,2:T(4,128)(2,1)}, bf16[2,4,10,1,256]{4,1,0,3,2:T(4,128)(2,1)}, u32[]{:S(2)}, u32[]{:S(2)}) collective-permute-start(bf16[2,4,10,1,256]{4,1,0,3,2:T(4,128)(2,1)} %get-tuple-element.25), channel_id=1, source_target_pairs={{0,1},{2,3},{4,5},{6,7},{8,9},{10,11},{12,13},{14,15},{16,17},{18,... | collective-permute-start | bytes 122888 | tf_op jit(solution)/shard_map/ppermute | solution.py:19
  23.0 43.5 %collective-permute-start.4 = (bf16[2,4,10,1,256]{4,1,0,3,2:T(4,128)(2,1)}, bf16[2,4,10,1,256]{4,1,0,3,2:T(4,128)(2,1)}, u32[]{:S(2)}, u32[]{:S(2)}) collective-permute-start(bf16[2,4,10,1,256]{4,1,0,3,2:T(4,128)(2,1)} %get-tuple-element.26), channel_id=1, source_target_pairs={{1,0},{3,2},{5,4},{7,6},{9,8},{11,10},{13,12},{15,14},{17,16},{19,... | collective-permute-start | bytes 122888 | tf_op jit(solution)/shard_map/ppermute | solution.py:22
  24.8 0.9 copy-start.12
  24.8 0.9 copy-start.13
  24.9 1.1 copy-start.10
  24.9 1.1 copy-start.11
  25.1 1.2 copy-start.8
  25.1 1.2 copy-start.9
  25.2 1.2 copy-start.24
  25.2 1.2 copy-start.25
  26.0 0.7 copy-start.22
  26.0 0.7 copy-start.23
  26.4 0.7 copy-start.18
  26.4 0.7 copy-start.19
  26.4 0.7 copy-start.20
  26.4 0.7 copy-start.21
  26.7 0.7 copy-start.14
  26.8 0.7 copy-start.15
  26.8 0.7 copy-start.16
  49.4 5.9 %copy-start = (bf16[2,16,8,8,256]{4,3,2,1,0:T(8,128)(2,1)S(1)}, bf16[2,16,8,8,256]{4,3,2,1,0:T(8,128)(2,1)}, u32[]{:S(2)}) copy-start(bf16[2,16,8,8,256]{4,3,2,1,0:T(8,128)(2,1)} %param.6) | copy-start | bytes 3145732
  56.8 9.7 %copy-start.3 = (bf16[2,4,10,8,256]{4,1,0,3,2:T(4,128)(2,1)S(1)}, bf16[2,4,10,8,256]{4,1,0,3,2:T(4,128)(2,1)}, u32[]{:S(2)}) copy-start(bf16[2,4,10,8,256]{4,1,0,3,2:T(4,128)(2,1)} %copy-done.2) | copy-start | bytes 983044
  61.7 35.3 %collective-permute-start.5 = (bf16[1,16,1,16,256]{4,3,2,1,0:T(8,128)(2,1)S(1)}, bf16[1,16,1,16,256]{4,3,2,1,0:T(8,128)(2,1)S(1)}, u32[]{:S(2)}, u32[]{:S(2)}) collective-permute-start(bf16[1,16,1,16,256]{4,3,2,1,0:T(8,128)(2,1)S(1)} %slice.448), channel_id=1, source_target_pairs={{0,2},{2,4},{4,6},{6,8},{8,10},{10,12},{12,14},{1,3},{3,5},{5,7},{... | collective-permute-start | bytes 393224 | tf_op jit(solution)/shard_map/ppermute | solution.py:30
  70.3 1.7 copy-start.5
  80.2 1.7 copy-start.1
  164.7 2.2 %copy-start.26 = (f32[32]{0:T(128)S(1)}, f32[32]{0:T(128)}, u32[]{:S(2)}) copy-start(f32[32]{0:T(128)} %get-tuple-element.12) | copy-start | bytes 388
  (1 other events, 0.7 us)
